TPU v7x, 32 devices: a whole 2x2x4 slice. The times are simulated.
32 devices in a mesh: row: 8 (over z, y), col: 4 (over x, core).
Axes of the slice: x: 2, y: 2, z: 4, core: 2. Of those that a mesh axis runs over, the one named last changes fastest.
Arguments:
- image_states: bfloat16 [64, 3072], P(('row', 'col')), may hold values from -6 to 6
- latent: float32 [64, 64], P(('row', 'col')), may hold values from -6 to 6
- text_keys: bfloat16 [1024, 3072], P('row', 'col')
- text_values: bfloat16 [1024, 3072], P('row', 'col'), may hold values from -6 to 6
- mod_table: float32 [4, 8, 3072], replicated, may hold values from -3 to 3
- timestep: int32 [4], replicated, may hold values from 0 to 3
- grid_size: int32 [4, 2], replicated, may hold values from 1 to 8, as said below
- rope_offset: int32 [4, 2], replicated, may hold values from 0 to 63
- w_qkv: bfloat16 [3072, 9216], P(None, 'row'), may hold values from -0.109375 to 0.109375
- q_gain: float32 [128], replicated, may hold values from 0.1 to 1.9
- k_gain: float32 [128], replicated, may hold values from 0.5 to 4
- w_out: bfloat16 [3072, 3072], P('col', 'row'), may hold values from -0.109375 to 0.109375
- w_fc1: bfloat16 [3072, 12288], P(None, 'row'), may hold values from -0.109375 to 0.109375
- w_fc2: bfloat16 [12288, 3072], P('row'), may hold values from -0.0546875 to 0.0546875
- w_final: bfloat16 [3072, 64], replicated, may hold values from -0.109375 to 0.109375
Outputs:
- velocity: float32 [64, 64], P(('row', 'col'))
- next_latent: float32 [64, 64], P(('row', 'col'))
Inputs may be any that keep to these rules, and one draw needn't show every extreme that they name: `grid_size`: column 0 is a request's grid height, at most 2; column 1 its grid width, at most 8; in every draw some request has height 2 and some request width 8.
All inputs are finite; a program needn't handle non-finite values.
Results may differ from a plain program's by a relative error of at most 0.008.
Values may be sent and summed in bfloat16 or wider, within the bound.
No kernel may reach another device: no remote copies, remote signals or barrier semaphores. Data moves between devices by JAX's collectives and lax.ppermute only.
A program may use at most 128 MiB of HBM per device.

v0:
```python
import jax
import jax.numpy as jnp
from jax import lax
from jax.sharding import PartitionSpec as P

REQ = 4
TXT = 256
STEPS = 4
eps_norm = 1e-06
blend = 0.25
mask_floor = -1e30


def with_halo(cells, sides, width):
    for axis, dim in sides:
        count = lax.axis_size(axis)
        ends = count - 1
        head = lax.slice_in_dim(cells, 0, width, axis=dim)
        tail = lax.slice_in_dim(cells, cells.shape[dim] - width, cells.shape[dim], axis=dim)
        cells = jnp.concatenate(
            [
                lax.ppermute(tail, axis, [(i, (i + 1) % count) for i in range(ends)]),
                cells,
                lax.ppermute(head, axis, [((i + 1) % count, i) for i in range(ends)]),
            ],
            axis=dim,
        )
    return cells


def layer_norm(values):
    mean_value = jnp.mean(values, -1, keepdims=True)
    centred = values - mean_value
    return centred * lax.rsqrt(jnp.mean(centred * centred, -1, keepdims=True) + eps_norm)


def modulate(values, shift_vec, scale_vec):
    return (layer_norm(values) * (1.0 + scale_vec) + shift_vec).astype(jnp.bfloat16)


def rope_tables(pos_h, pos_w, head_size):
    time_half = head_size // 16
    axis_dim = (head_size - head_size // 8) // 2
    freq_index = jnp.arange(axis_dim // 2, dtype=jnp.float32)
    frequency = 10000.0 ** (-2.0 * freq_index / axis_dim)
    angles = jnp.concatenate(
        [
            jnp.zeros((pos_h.shape[0], time_half), jnp.float32),
            pos_h[:, None] * frequency[None, :],
            pos_w[:, None] * frequency[None, :],
        ],
        1,
    )
    return (jnp.cos(angles), jnp.sin(angles))


def norm_rope(values, gain_vec, cosine_table, sine_table, head_count, head_size):
    row_total = values.shape[0]
    per_head = values.astype(jnp.float32).reshape(row_total, head_count, head_size)
    per_head = (
        per_head * lax.rsqrt(jnp.mean(per_head * per_head, -1, keepdims=True) + eps_norm) * gain_vec
    )
    paired = per_head.reshape(row_total, head_count, head_size // 2, 2)
    even_part = paired[..., 0]
    odd_part = paired[..., 1]
    cos_wide = cosine_table[:, None, :]
    sin_wide = sine_table[:, None, :]
    turned = jnp.stack(
        [even_part * cos_wide - odd_part * sin_wide, even_part * sin_wide + odd_part * cos_wide], -1
    )
    return turned.reshape(row_total, head_count * head_size).astype(jnp.bfloat16)


def on_device(
    image_states,
    latent,
    text_keys,
    text_values,
    mod_table,
    timestep,
    grid_size,
    rope_offset,
    w_qkv,
    q_gain,
    k_gain,
    w_out,
    w_fc1,
    w_fc2,
    w_final,
):
    col_total = lax.axis_size("col")
    row_pos = lax.axis_index("row")
    col_pos = lax.axis_index("col")
    tile_w = image_states.shape[0]
    width = image_states.shape[1]
    head_size = q_gain.shape[0]
    head_count = width // head_size
    local_heads = head_count // col_total
    request = row_pos % REQ
    grid_row = row_pos // REQ
    grid_col = col_pos * tile_w + jnp.arange(tile_w, dtype=jnp.int32)
    req_slots = jnp.arange(REQ, dtype=jnp.int32)
    req_onehot = req_slots == request
    limits = jnp.sum(jnp.where(req_onehot[:, None], grid_size, 0), 0)
    offsets = jnp.sum(jnp.where(req_onehot[:, None], rope_offset, 0), 0)
    step_now = jnp.sum(jnp.where(req_onehot, timestep, 0))
    token_ok = (grid_row < limits[0]) & (grid_col < limits[1])
    modulation = lax.dynamic_index_in_dim(mod_table, step_now, 0, keepdims=False)
    states = image_states.astype(jnp.float32)
    normed = modulate(states, modulation[0], modulation[1])
    joined_cols = jnp.dot(
        lax.all_gather(normed, "row", axis=0, tiled=True), w_qkv, preferred_element_type=jnp.float32
    ).astype(jnp.bfloat16)
    joined = lax.all_to_all(joined_cols, "row", split_axis=0, concat_axis=1, tiled=True)
    pos_h = jnp.zeros((tile_w,), jnp.float32) + (grid_row + offsets[0]).astype(jnp.float32)
    pos_w = (grid_col + offsets[1]).astype(jnp.float32)
    cosine_table, sine_table = rope_tables(pos_h, pos_w, head_size)
    queries = norm_rope(joined[:, :width], q_gain, cosine_table, sine_table, head_count, head_size)
    image_keys = norm_rope(
        joined[:, width : 2 * width], k_gain, cosine_table, sine_table, head_count, head_size
    )
    q_heads, k_heads, v_heads = (
        lax.all_to_all(queries, "col", split_axis=1, concat_axis=0, tiled=True),
        lax.all_to_all(image_keys, "col", split_axis=1, concat_axis=0, tiled=True),
        lax.all_to_all(joined[:, 2 * width :], "col", split_axis=1, concat_axis=0, tiled=True),
    )
    image_rows = k_heads.shape[0]
    text_rows = text_keys.shape[0]
    shard_rows = image_rows + text_rows
    q_block = q_heads.reshape(image_rows, local_heads, head_size)
    key_rows = jnp.concatenate([k_heads, text_keys], 0)
    value_rows = jnp.concatenate([v_heads, text_values], 0)
    run_max = jnp.full((image_rows, local_heads), mask_floor, jnp.float32)
    key_piece = lax.all_gather(key_rows, "row", axis=0, tiled=True)
    value_piece = lax.all_gather(value_rows, "row", axis=0, tiled=True)
    piece_rows = key_piece.shape[0]
    global_row = jnp.arange(piece_rows, dtype=jnp.int32)
    shard_id = global_row // shard_rows
    within = global_row % shard_rows
    is_image = within < image_rows
    source_col = within // tile_w
    source_cell = within % tile_w
    image_req = shard_id % REQ
    text_req = (shard_id * text_rows + within - image_rows) // TXT
    key_req = jnp.where(is_image, image_req, text_req)
    key_onehot = key_req[:, None] == req_slots[None, :]
    key_height = jnp.sum(jnp.where(key_onehot, grid_size[:, 0][None, :], 0), 1)
    key_width = jnp.sum(jnp.where(key_onehot, grid_size[:, 1][None, :], 0), 1)
    image_ok = (shard_id // REQ < key_height) & (source_col * tile_w + source_cell < key_width)
    key_ok = (key_req == request) & (jnp.logical_not(is_image) | image_ok)
    scores = jnp.einsum(
        "qhd,khd->qhk",
        q_block,
        key_piece.reshape(piece_rows, local_heads, head_size),
        preferred_element_type=jnp.float32,
    ) * head_size ** (-0.5)
    new_max = jnp.maximum(run_max, jnp.max(jnp.where(key_ok, scores, mask_floor), -1))
    weights = jnp.where(key_ok, jnp.exp(scores - new_max[..., None]), 0.0)
    new_sum = jnp.sum(weights, -1)
    new_acc = jnp.einsum(
        "qhk,khd->qhd",
        weights.astype(jnp.bfloat16),
        value_piece.reshape(piece_rows, local_heads, head_size),
        preferred_element_type=jnp.float32,
    )
    mixed = (
        (new_acc / new_sum[..., None])
        .astype(jnp.bfloat16)
        .reshape(image_rows, local_heads * head_size)
    )
    partial_out = jnp.dot(
        mixed, lax.all_gather(w_out, "row", axis=1, tiled=True), preferred_element_type=jnp.float32
    )
    attended = lax.psum_scatter(
        partial_out.astype(jnp.bfloat16), "col", scatter_dimension=0, tiled=True
    ).astype(jnp.float32)
    first_res = (states + modulation[2] * attended).astype(jnp.bfloat16)
    normed_two = modulate(first_res.astype(jnp.float32), modulation[3], modulation[4])
    all_rows = lax.all_gather(normed_two, "row", axis=0, tiled=True)
    hidden = jax.nn.gelu(
        jnp.dot(all_rows, w_fc1, preferred_element_type=jnp.float32), approximate=True
    ).astype(jnp.bfloat16)
    every_term = jnp.dot(hidden, w_fc2, preferred_element_type=jnp.float32)
    every_sum = lax.psum(every_term, "row")
    mlp_out = lax.dynamic_slice_in_dim(every_sum, row_pos * tile_w, tile_w, 0)
    second_res = first_res.astype(jnp.float32) + modulation[5] * mlp_out
    normed_three = modulate(second_res, modulation[6], modulation[7])
    raw_velocity = jnp.dot(normed_three, w_final, preferred_element_type=jnp.float32)
    masked = jnp.where(token_ok[:, None], raw_velocity, 0.0)
    padded = with_halo(masked, (("col", 0),), 1)
    left_side = padded[:-2]
    right_side = padded[2:]
    velocity = jnp.where(
        token_ok[:, None], masked + blend * (left_side + right_side - 2.0 * masked), 0.0
    )
    next_latent = latent + -1.0 / STEPS * velocity
    return (velocity, next_latent)


def solution(mesh):
    placed = (
        P(("row", "col"), None),
        P(("row", "col"), None),
        P("row", "col"),
        P("row", "col"),
        P(),
        P(),
        P(),
        P(),
        P(None, "row"),
        P(),
        P(),
        P("col", "row"),
        P(None, "row"),
        P("row", None),
        P(),
    )
    return jax.shard_map(
        on_device,
        mesh=mesh,
        in_specs=placed,
        out_specs=(P(("row", "col"), None), P(("row", "col"), None)),
        check_vma=False,
    )
```

profile of v0, /device:TPU:1, one launch (start us, length us, event | category | flops | bytes accessed | tf_op | source)
XLA Modules:
  0.0 413.6 jit_solution(1863781639350607465)
XLA Ops:
  7.2 1.3 select_reduce_fusion.5
  9.8 0.8 convert_reduce_fusion.1
  10.7 0.9 fusion.36
  12.3 2.2 dynamic-slice_add_fusion
  14.5 0.8 fusion.50
  15.3 25.6 %all-gather = bf16[8,2,3072]{2,1,0:T(2,128)(2,1)S(1)} all-gather(bf16[1,2,3072]{2,1,0:T(2,128)(2,1)S(1)} %fusion.50), channel_id=1, replica_groups=mesh['row'=8,'col'=4] {'row'}, dimensions={0}, use_global_device_ids=true | all-gather | bytes 110592 | tf_op jit(solution)/shard_map/all_gather | solution.py:112
  41.0 4.0 convolution_convert_fusion.1
  45.7 5.0 %all-to-all-start = ((bf16[8,2,1152]{2,1,0:T(2,128)(2,1)}), bf16[8,2,1152]{2,1,0:T(2,128)(2,1)S(1)}, u32[]{:S(2)}, u32[]{:S(2)}) async-start(bf16[8,2,1152]{2,1,0:T(2,128)(2,1)} %all_to_all.50), calls=%async_computation | async-start | bytes 73728 | tf_op jit(solution)/shard_map/all_to_all | solution.py:114
  53.2 0.7 mul.324
  53.9 0.7 mul.306
  54.7 1.6 all-to-all-done
  56.9 1.5 reshape.266
  59.2 2.3 reshape.264
  62.2 1.0 multiply_multiply_fusion
  63.3 5.2 %slice_multiply_fusion.5 = (f32[2,24,64,1]{3,2,1,0:T(8,128)}, f32[2,24,64,1]{3,2,1,0:T(8,128)}, f32[2,24,64,1]{3,2,1,0:T(8,128)}, f32[2,24,64,1]{3,2,1,0:T(8,128...) fusion(f32[2,24,64,2]{3,2,1,0:T(8,128)S(1)} %multiply_multiply_, ...), kind=kLoop, calls=%fused_computation.11 | loop fusion | flops 24576 | bytes 148480 | tf_op jit(solution)/shard_map/mul | solution.py:69
  68.5 2.5 copy.52
  71.1 2.5 copy.53
  73.6 2.5 copy.54
  76.1 2.5 copy.55
  78.6 0.8 subtract_convert_fusion.1
  79.4 0.8 add_convert_fusion.2
  80.8 2.0 copy.56
  82.8 2.1 convert_element_type.69
  84.9 14.5 %all_to_all.67 = bf16[2,4,768]{2,0,1:T(2,128)(2,1)} all-to-all(bf16[2,4,768]{2,0,1:T(2,128)(2,1)S(1)} %copy.57), channel_id=1, replica_groups=mesh['row'=8,'col'=4] {'col'}, dimensions={1} | all-to-all | bytes 24576 | tf_op jit(solution)/shard_map/all_to_all | solution.py:124
  100.1 1.6 pad_maximum_fusion.1
  101.8 7.8 %all_to_all.68 = bf16[2,4,768]{2,0,1:T(2,128)(2,1)} all-to-all(bf16[2,4,768]{2,0,1:T(2,128)(2,1)} %bitcast.72), channel_id=1, replica_groups=mesh['row'=8,'col'=4] {'col'}, dimensions={1} | all-to-all | bytes 24576 | tf_op jit(solution)/shard_map/all_to_all | solution.py:125
  110.3 1.6 pad_maximum_fusion
  112.8 2.5 copy.59
  115.4 2.5 copy.60
  117.9 1.1 copy.61
  120.2 1.1 convert_element_type.71
  121.9 3.9 all-to-all-start.3
  127.2 2.2 all-to-all-done.3
  129.4 14.7 %all-gather.8.cloned.1.call-done = bf16[1088,768]{1,0:T(8,128)(2,1)} async-done(((bf16[136,768]{1,0:T(8,128)(2,1)}), bf16[1088,768]{1,0:T(8,128)(2,1)}) %all-gather.8.cloned.1.call-update) | async-done | bytes 1671184 | tf_op jit(solution)/shard_map/all_gather | solution.py:134
  144.1 3.8 copy.58
  147.9 42.3 %all-gather.6.cloned.1.call-done = bf16[1088,768]{1,0:T(8,128)(2,1)} async-done(((bf16[136,768]{1,0:T(8,128)(2,1)}), bf16[1088,768]{1,0:T(8,128)(2,1)}) %all-gather.6.cloned.1.call-update) | async-done | bytes 1671184 | tf_op jit(solution)/shard_map/all_gather | solution.py:135
  190.2 2.7 copy.51
  192.9 1.9 select_reduce_fusion
  195.0 77.3 %all-gather.10.cloned.1.call-done = bf16[768,3072]{1,0:T(8,128)(2,1)} async-done(((bf16[768,384]{1,0:T(8,128)(2,1)}), bf16[768,3072]{1,0:T(8,128)(2,1)}) %all-gather.10.cloned.1.call-update) | async-done | bytes 4718608 | tf_op jit(solution)/shard_map/all_gather | solution.py:172
  272.3 3.7 convolution_convert_fusion
  276.0 11.2 %all-reduce = bf16[8,3072]{1,0:T(8,128)(2,1)S(1)} all-reduce(bf16[8,3072]{1,0:T(8,128)(2,1)S(1)} %convolution_convert_fusion), channel_id=2, replica_groups=mesh['row'=8,'col'=4] {'col'}, use_global_device_ids=true, to_apply=%region_11.12.clone | all-reduce | flops 24576 | bytes 98304
  287.7 24.4 %all-gather.1 = bf16[8,2,3072]{2,1,0:T(2,128)(2,1)S(1)} all-gather(bf16[1,2,3072]{2,1,0:T(2,128)(2,1)S(1)} %fusion.51), channel_id=1, replica_groups=mesh['row'=8,'col'=4] {'row'}, dimensions={0}, use_global_device_ids=true | all-gather | bytes 110592 | tf_op jit(solution)/shard_map/all_gather | solution.py:179
  312.2 9.6 %fusion.22 = f32[16,3072]{1,0:T(8,128)} fusion(bf16[1536,3072]{1,0:T(8,128)(2,1)} %param.28, bf16[16,3072]{1,0:T(8,128)(2,1)S(1)} %reshape.272, bf16[3072,1536]{1,0:T(8,128)(2,1)} %param.27), kind=kOutput, calls=%fused_computation.37 | convolution fusion | flops 302211072 | bytes 19169280 | tf_op jit(solution)/shard_map/dot_general | solution.py:183
  323.0 71.4 %all-reduce.3.cloned.1.call-done = f32[16,3072]{1,0:T(8,128)} async-done(((f32[16,3072]{1,0:T(8,128)}), f32[16,3072]{1,0:T(8,128)}) %all-reduce.3.cloned.1.call-update) | async-done | bytes 196624 | tf_op jit(solution)/shard_map/psum | solution.py:184
  394.4 1.0 fusion.82
  396.0 5.6 %collective-permute-start = (f32[1,64]{1,0:T(1,128)S(1)}, f32[1,64]{1,0:T(1,128)S(1)}, u32[]{:S(2)}, u32[]{:S(2)}) collective-permute-start(f32[1,64]{1,0:T(1,128)S(1)} %get-tuple-element.45), channel_id=1, source_target_pairs={{0,1},{1,2},{2,3},{4,5},{5,6},{6,7},{8,9},{9,10},{10,11},{12,13},{... | collective-permute-start | bytes 776 | tf_op jit(solution)/shard_map/ppermute | solution.py:22
  401.5 1.9 collective-permute-start.1
  403.5 2.9 collective-permute-done.1
  (97 shorter events, 12.7 us)
Async XLA Ops:
  7.2 388.5 %copy-start = (bf16[3072,64]{0,1:T(8,128)(2,1)S(1)}, bf16[3072,64]{0,1:T(8,128)(2,1)}, u32[]{:S(2)}) copy-start(bf16[3072,64]{0,1:T(8,128)(2,1)} %param.29) | copy-start | bytes 1179652
  41.0 9.8 %copy-start.12 = (s32[4,2]{0,1:T(2,128)S(1)}, s32[4,2]{0,1:T(2,128)}, u32[]{:S(2)}) copy-start(s32[4,2]{0,1:T(2,128)} %param.21) | copy-start | bytes 100
  41.0 9.8 %copy-start.13 = (s32[4,2]{0,1:T(2,128)S(1)}, s32[4,2]{0,1:T(2,128)}, u32[]{:S(2)}) copy-start(s32[4,2]{0,1:T(2,128)} %param.22) | copy-start | bytes 100
  41.0 12.1 %copy-start.15 = (f32[128]{0:T(128)S(1)}, f32[128]{0:T(128)}, u32[]{:S(2)}) copy-start(f32[128]{0:T(128)} %param.24) | copy-start | bytes 1540
  41.0 12.9 %copy-start.16 = (f32[128]{0:T(128)S(1)}, f32[128]{0:T(128)}, u32[]{:S(2)}) copy-start(f32[128]{0:T(128)} %param.25) | copy-start | bytes 1540
  45.7 10.6 %all-to-all-start = ((bf16[8,2,1152]{2,1,0:T(2,128)(2,1)}), bf16[8,2,1152]{2,1,0:T(2,128)(2,1)S(1)}, u32[]{:S(2)}, u32[]{:S(2)}) async-start(bf16[8,2,1152]{2,1,0:T(2,128)(2,1)} %all_to_all.50), calls=%async_computation | async-start | bytes 73728 | tf_op jit(solution)/shard_map/all_to_all | solution.py:114
  50.7 93.4 %all-gather.8.cloned.1.call-start = ((), (), s32[]{:S(2)}) async-start(), calls=%async_computation.5 | async-start | bytes 1880064 | tf_op jit(solution)/shard_map/all_gather | solution.py:134
  62.2 1.0 copy-start.2
  101.8 88.4 %all-gather.6.cloned.1.call-start = ((), (), s32[]{:S(2)}) async-start(), calls=%async_computation.4 | async-start | bytes 1880064 | tf_op jit(solution)/shard_map/all_gather | solution.py:135
  111.9 160.4 %all-gather.10.cloned.1.call-start = ((), (), s32[]{:S(2)}) async-start(), calls=%async_computation.6 | async-start | bytes 5308416 | tf_op jit(solution)/shard_map/all_gather | solution.py:172
  119.0 0.7 copy-start.3
  119.0 0.8 copy-start.4
  119.0 0.8 copy-start.5
  119.0 6.9 %copy-start.17 = (u32[32]{0:T(128)S(1)}, u32[32]{0:T(128)}, u32[]{:S(2)}) copy-start(u32[32]{0:T(128)} %constant.158) | copy-start | bytes 388
  121.9 7.5 %all-to-all-start.3 = ((bf16[2,4,768]{2,0,1:T(2,128)(2,1)}), bf16[2,4,768]{2,0,1:T(2,128)(2,1)S(1)}, u32[]{:S(2)}, u32[]{:S(2)}) async-start(bf16[2,4,768]{2,0,1:T(2,128)(2,1)} %copy.64), calls=%async_computation.3 | async-start | bytes 24576 | tf_op jit(solution)/shard_map/all_to_all | solution.py:123
  125.9 268.5 %all-reduce.3.cloned.1.call-start = ((), (), s32[]{:S(2)}) async-start(), calls=%async_computation.7 | async-start | bytes 393216 | tf_op jit(solution)/shard_map/psum | solution.py:184
  272.3 14.9 %copy-start.1 = (bf16[2,3072]{1,0:T(2,128)(2,1)S(1)}, bf16[2,3072]{1,0:T(2,128)(2,1)}, u32[]{:S(2)}) copy-start(bf16[2,3072]{1,0:T(2,128)(2,1)} %param.15) | copy-start | bytes 36868
  272.3 14.9 %copy-start.9 = (f32[1,1,3072]{2,1,0:T(1,128)S(1)}, f32[1,1,3072]{2,1,0:T(1,128)}, u32[]{:S(2)}) copy-start(f32[1,1,3072]{2,1,0:T(1,128)} %get-tuple-element.30) | copy-start | bytes 36868
  272.3 15.3 %copy-start.7 = (f32[1,1,3072]{2,1,0:T(1,128)S(1)}, f32[1,1,3072]{2,1,0:T(1,128)}, u32[]{:S(2)}) copy-start(f32[1,1,3072]{2,1,0:T(1,128)} %get-tuple-element.25) | copy-start | bytes 36868
  272.3 15.3 %copy-start.8 = (f32[1,1,3072]{2,1,0:T(1,128)S(1)}, f32[1,1,3072]{2,1,0:T(1,128)}, u32[]{:S(2)}) copy-start(f32[1,1,3072]{2,1,0:T(1,128)} %get-tuple-element.26) | copy-start | bytes 36868
  312.1 82.3 %copy-start.6 = (f32[1,1,3072]{2,1,0:T(1,128)S(1)}, f32[1,1,3072]{2,1,0:T(1,128)}, u32[]{:S(2)}) copy-start(f32[1,1,3072]{2,1,0:T(1,128)} %get-tuple-element.27) | copy-start | bytes 36868
  312.1 83.6 %copy-start.10 = (f32[1,1,3072]{2,1,0:T(1,128)S(1)}, f32[1,1,3072]{2,1,0:T(1,128)}, u32[]{:S(2)}) copy-start(f32[1,1,3072]{2,1,0:T(1,128)} %get-tuple-element.24) | copy-start | bytes 36868
  312.1 83.6 %copy-start.11 = (f32[1,1,3072]{2,1,0:T(1,128)S(1)}, f32[1,1,3072]{2,1,0:T(1,128)}, u32[]{:S(2)}) copy-start(f32[1,1,3072]{2,1,0:T(1,128)} %get-tuple-element.31) | copy-start | bytes 36868
  312.1 94.3 %copy-start.14 = (f32[2,64]{1,0:T(2,128)S(1)}, f32[2,64]{1,0:T(2,128)}, u32[]{:S(2)}) copy-start(f32[2,64]{1,0:T(2,128)} %param.16) | copy-start | bytes 1540
  396.0 7.5 %collective-permute-start = (f32[1,64]{1,0:T(1,128)S(1)}, f32[1,64]{1,0:T(1,128)S(1)}, u32[]{:S(2)}, u32[]{:S(2)}) collective-permute-start(f32[1,64]{1,0:T(1,128)S(1)} %get-tuple-element.45), channel_id=1, source_target_pairs={{0,1},{1,2},{2,3},{4,5},{5,6},{6,7},{8,9},{9,10},{10,11},{12,13},{... | collective-permute-start | bytes 776 | tf_op jit(solution)/shard_map/ppermute | solution.py:22
  401.5 4.9 %collective-permute-start.1 = (f32[1,64]{1,0:T(1,128)S(1)}, f32[1,64]{1,0:T(1,128)S(1)}, u32[]{:S(2)}, u32[]{:S(2)}) collective-permute-start(f32[1,64]{1,0:T(1,128)S(1)} %get-tuple-element.46), channel_id=1, source_target_pairs={{1,0},{2,1},{3,2},{5,4},{6,5},{7,6},{9,8},{10,9},{11,10},{13,12},{... | collective-permute-start | bytes 776 | tf_op jit(solution)/shard_map/ppermute | solution.py:24
Sparse Core Ops, SparseCore 0:
  101.9 42.1 all-gather.7
  146.3 43.8 all-gather.5
  192.3 79.9 all-gather.9
  321.9 72.4 all-reduce.2
where the time goes:
time: 415 us; the launch traced here: 414 us
  waiting for transfers between devices  213 us (51%)
  blocking collectives  83.5 us (20%)
  local copies, waits for them, and re-layouts  38.6 us (9%)
  other arithmetic  24.4 us (6%)
  matrix products  19.5 us (5%)
  between operations  18 us (4%)
  starting transfers between devices  16.5 us (4%)
    all_gather x1, waiting for transfers between devices, on_device(): lax.all_gather(w_out, 'row', axis=1, tiled=True)  77.3 us
    psum x1, waiting for transfers between devices, on_device(): every_sum = lax.psum(every_term, 'row')  71.4 us
    all_gather x1, waiting for transfers between devices, on_device(): value_piece = lax.all_gather(value_rows, 'row', axis=0, tiled=True)  42.3 us
    all_gather x1, blocking collectives, on_device(): lax.all_gather(normed, 'row', axis=0, tiled=True)  25.6 us
    all_gather x1, blocking collectives, on_device(): all_rows = lax.all_gather(normed_two, 'row', axis=0, tiled=True)  24.4 us
    all_gather x1, waiting for transfers between devices, on_device(): key_piece = lax.all_gather(key_rows, 'row', axis=0, tiled=True)  14.7 us
    all_to_all x1, blocking collectives, on_device(): lax.all_to_all(image_keys, 'col', split_axis=1, concat_axis=0, tiled=True)  14.5 us
    unnamed x1, blocking collectives  11.2 us
  transfers between devices with their start and end apart: 8, of which 7 were waited for; matrix products, arithmetic and copies ran while one was open for 6% of the time, Pallas kernels for 0%

commit v1 on v0

--- a/solution.py
+++ b/solution.py
@@ -1,7 +1,9 @@
+import functools
 import jax
 import jax.numpy as jnp
 from jax import lax
 from jax.sharding import PartitionSpec as P
+from jax.lax import axis_index, axis_size, ppermute
 
 REQ = 4
 TXT = 256
@@ -9,6 +11,27 @@
 eps_norm = 1e-06
 blend = 0.25
 mask_floor = -1e30
+
+
+def settle_ways(xs, axis_name):
+    cores_n = axis_size(axis_name)
+    runs = []
+    for u in range(cores_n):
+        runs.append((u, (u + 1) % cores_n))
+    shelf = []
+    for u in range(cores_n):
+        shelf.append((u, (u - 1) % cores_n))
+    big, piece_out = ([xs], [xs])
+    for _ in range(cores_n // 2):
+        big.append(ppermute(big[-1], axis_name, runs))
+    for _ in range((cores_n - 1) // 2):
+        piece_out.append(ppermute(piece_out[-1], axis_name, shelf))
+    local_now = jnp.concatenate([*big[::-1], *piece_out[1:]], axis=0)
+    next_value = jnp.roll(local_now, (axis_index(axis_name) - cores_n // 2) * xs.shape[0], axis=0)
+    return next_value
+
+
+find_sample = functools.partial(settle_ways, axis_name="row")
 
 
 def with_halo(cells, sides, width):
@@ -132,7 +155,7 @@
     value_rows = jnp.concatenate([v_heads, text_values], 0)
     run_max = jnp.full((image_rows, local_heads), mask_floor, jnp.float32)
     key_piece = lax.all_gather(key_rows, "row", axis=0, tiled=True)
-    value_piece = lax.all_gather(value_rows, "row", axis=0, tiled=True)
+    value_piece = find_sample(value_rows)
     piece_rows = key_piece.shape[0]
     global_row = jnp.arange(piece_rows, dtype=jnp.int32)
     shard_id = global_row // shard_rows

time: 415 us -> 387 us (0.933)
  waiting for transfers between devices: 213 us -> 161 us
  starting transfers between devices: 16.5 us -> 38.5 us
  blocking collectives: 83.5 us -> 75.8 us
  local copies, waits for them, and re-layouts: 38.6 us -> 45.6 us
    all_gather x1 -> x0, waiting for transfers between devices: 42.3 us -> none  [on_device(): value_piece = lax.all_gather(value_rows, 'row', axis=0, tiled=True)]
    ppermute x0 -> x7, waiting for transfers between devices: none -> 16.4 us  [the longest x3 8.86 us: settle_ways(): piece_out.append(ppermute(piece_out[-1], axis_name, shelf))]
    all_gather x1, waiting for transfers between devices: 14.7 us -> 0.02 us  [on_device(): key_piece = lax.all_gather(key_rows, 'row', axis=0, tiled=True)]
    ppermute x0 -> x7, starting transfers between devices: none -> 12.2 us  [the longest x3 11 us: settle_ways(): piece_out.append(ppermute(piece_out[-1], axis_name, shelf))]
    all_gather x1, waiting for transfers between devices: 77.3 us -> 65.5 us  [on_device(): lax.all_gather(w_out, 'row', axis=1, tiled=True)]
    all_to_all x1 -> x0, blocking collectives: 7.75 us -> none  [on_device(): lax.all_to_all(joined[:, 2 * width:], 'col', split_axis=1, concat_axis=0,...]
    all_to_all x1, starting transfers between devices: 3.94 us -> 9.81 us  [on_device(): lax.all_to_all(queries, 'col', split_axis=1, concat_axis=0, tiled=True)]
    dynamic_slice x0 -> x2, local copies, waits for them, and re-layouts: none -> 4.38 us  [settle_ways(): jnp.roll(local_now, (axis_index(axis_name) - cores_n // 2) * xs.shape[0],...]
  transfers between devices with their start and end apart: 8 -> 15, of which waited for: 7 -> 10; matrix products, arithmetic and copies ran while one was open for 6% -> 8% of each run, Pallas kernels for 0% -> 0%
where the time goes in v1:
time: 387 us; the launch traced here: 385 us
  waiting for transfers between devices  161 us (42%)
  blocking collectives  75.8 us (20%)
  local copies, waits for them, and re-layouts  45.6 us (12%)
  starting transfers between devices  38.5 us (10%)
  other arithmetic  26.2 us (7%)
  matrix products  19.5 us (5%)
  between operations  18.2 us (5%)
    psum x1, waiting for transfers between devices, on_device(): every_sum = lax.psum(every_term, 'row')  71.4 us
    all_gather x1, waiting for transfers between devices, on_device(): lax.all_gather(w_out, 'row', axis=1, tiled=True)  65.5 us
    all_gather x1, blocking collectives, on_device(): lax.all_gather(normed, 'row', axis=0, tiled=True)  25.6 us
    all_gather x1, blocking collectives, on_device(): all_rows = lax.all_gather(normed_two, 'row', axis=0, tiled=True)  24.4 us
    all_to_all x1, blocking collectives, on_device(): lax.all_to_all(image_keys, 'col', split_axis=1, concat_axis=0, tiled=True)  14.5 us
    unnamed x1, blocking collectives  11.2 us
    ppermute x3, starting transfers between devices, settle_ways(): piece_out.append(ppermute(piece_out[-1], axis_name, shelf))  11 us
    all_to_all x1, starting transfers between devices, on_device(): lax.all_to_all(queries, 'col', split_axis=1, concat_axis=0, tiled=True)  9.81 us
  transfers between devices with their start and end apart: 15, of which 10 were waited for; matrix products, arithmetic and copies ran while one was open for 8% of the time, Pallas kernels for 0%

profile of v1, /device:TPU:1, one launch (start us, length us, event | category | flops | bytes accessed | tf_op | source)
XLA Modules:
  0.0 385.3 jit_solution(2982971903917605816)
XLA Ops:
  7.2 1.3 select_reduce_fusion.5
  12.3 2.2 dynamic-slice_add_fusion
  15.3 25.6 %all-gather = bf16[8,2,3072]{2,1,0:T(2,128)(2,1)S(1)} all-gather(bf16[1,2,3072]{2,1,0:T(2,128)(2,1)S(1)} %fusion.50), channel_id=1, replica_groups=mesh['row'=8,'col'=4] {'row'}, dimensions={0}, use_global_device_ids=true | all-gather | bytes 110592 | tf_op jit(solution)/shard_map/all_gather | solution.py:135
  41.0 4.0 %convolution_convert_fusion.1 = bf16[16,1152]{1,0:T(8,128)(2,1)S(1)} fusion(bf16[16,3072]{1,0:T(8,128)(2,1)S(1)} %reshape.270, bf16[3072,1152]{1,0:T(8,128)(2,1)} %param.23), kind=kOutput, calls=%fused_computation.3 | convolution fusion | flops 113264640 | bytes 7213056 | tf_op jit(solution)/shard_map/dot_general | solution.py:134
  45.7 5.0 %all-to-all-start = ((bf16[8,2,1152]{2,1,0:T(2,128)(2,1)}), bf16[8,2,1152]{2,1,0:T(2,128)(2,1)S(1)}, u32[]{:S(2)}, u32[]{:S(2)}) async-start(bf16[8,2,1152]{2,1,0:T(2,128)(2,1)} %all_to_all.50), calls=%async_computation | async-start | bytes 73728 | tf_op jit(solution)/shard_map/all_to_all | solution.py:137
  54.7 1.6 all-to-all-done
  57.0 1.5 reshape.266
  59.2 2.3 reshape.264
  64.1 5.2 %slice_multiply_fusion.5 = (f32[2,24,64,1]{3,2,1,0:T(8,128)}, f32[2,24,64,1]{3,2,1,0:T(8,128)}, f32[2,24,64,1]{3,2,1,0:T(8,128)}, f32[2,24,64,1]{3,2,1,0:T(8,128...) fusion(f32[2,24,64,2]{3,2,1,0:T(8,128)S(1)} %multiply_multiply_, ...), kind=kLoop, calls=%fused_computation.11 | loop fusion | flops 24576 | bytes 148480 | tf_op jit(solution)/shard_map/mul | solution.py:92
  69.3 2.5 copy.54
  71.9 2.5 copy.55
  74.4 2.5 copy.52
  76.9 2.5 copy.53
  81.6 2.0 copy.56
  83.6 2.1 convert_element_type.69
  85.7 14.5 %all_to_all.67 = bf16[2,4,768]{2,0,1:T(2,128)(2,1)} all-to-all(bf16[2,4,768]{2,0,1:T(2,128)(2,1)S(1)} %copy.57), channel_id=1, replica_groups=mesh['row'=8,'col'=4] {'col'}, dimensions={1} | all-to-all | bytes 24576 | tf_op jit(solution)/shard_map/all_to_all | solution.py:147
  101.0 1.6 pad_maximum_fusion
  103.4 3.9 %all-to-all-start.1 = ((bf16[2,4,768]{2,0,1:T(2,128)(2,1)}), bf16[2,4,768]{2,0,1:T(2,128)(2,1)S(1)}, u32[]{:S(2)}, u32[]{:S(2)}) async-start(bf16[2,4,768]{2,0,1:T(2,128)(2,1)} %bitcast.72), calls=%async_computation.1 | async-start | bytes 24576 | tf_op jit(solution)/shard_map/all_to_all | solution.py:148
  107.9 2.6 all-to-all-done.1
  112.4 1.6 constant_dynamic-update-slice_fusion
  114.2 1.4 select_reduce_fusion.1
  115.6 2.5 copy.61
  118.1 2.5 copy.62
  120.6 1.1 copy.59
  122.3 3.3 collective-permute-done
  126.4 4.2 %collective-permute-start.4 = (bf16[136,768]{1,0:T(8,128)(2,1)}, bf16[136,768]{1,0:T(8,128)(2,1)S(1)}, u32[]{:S(2)}, u32[]{:S(2)}) collective-permute-start(bf16[136,768]{1,0:T(8,128)(2,1)} %constant_dynamic-update-slice_fusion), channel_id=1, source_target_pairs={{0,28},{4,0},{8,4},{12,8},{16,12},{20,16},{24,20},{28,24},{1,29},{... | collective-permute-start | bytes 626696 | tf_op jit(solution)/shard_map/ppermute | solution.py:28
  130.6 4.2 %collective-permute-done.1 = bf16[136,768]{1,0:T(8,128)(2,1)S(1)} collective-permute-done((bf16[136,768]{1,0:T(8,128)(2,1)}, bf16[136,768]{1,0:T(8,128)(2,1)S(1)}, u32[]{:S(2)}, u32[]{:S(2)}) %collective-permute-start.1) | collective-permute-done | bytes 208928 | tf_op jit(solution)/shard_map/ppermute | solution.py:26
  134.8 1.0 collective-permute-start.2
  137.0 1.1 convert_element_type.71
  138.7 9.8 %all-to-all-start.3 = ((bf16[2,4,768]{2,0,1:T(2,128)(2,1)}), bf16[2,4,768]{2,0,1:T(2,128)(2,1)S(1)}, u32[]{:S(2)}, u32[]{:S(2)}) async-start(bf16[2,4,768]{2,0,1:T(2,128)(2,1)} %copy.64), calls=%async_computation.3 | async-start | bytes 24576 | tf_op jit(solution)/shard_map/all_to_all | solution.py:146
  148.5 2.0 collective-permute-start.5
  152.0 6.5 %collective-permute-done.5 = bf16[136,768]{1,0:T(8,128)(2,1)S(1)} collective-permute-done((bf16[136,768]{1,0:T(8,128)(2,1)S(1)}, bf16[136,768]{1,0:T(8,128)(2,1)S(1)}, u32[]{:S(2)}, u32[]{:S(2)}) %collective-permute-start.5) | collective-permute-done | bytes 208928 | tf_op jit(solution)/shard_map/ppermute | solution.py:28
  158.6 4.9 %collective-permute-start.6 = (bf16[136,768]{1,0:T(8,128)(2,1)S(1)}, bf16[136,768]{1,0:T(8,128)(2,1)S(1)}, u32[]{:S(2)}, u32[]{:S(2)}) collective-permute-start(bf16[136,768]{1,0:T(8,128)(2,1)S(1)} %collective-permute-done.5), channel_id=1, source_target_pairs={{0,28},{4,0},{8,4},{12,8},{16,12},{20,16},{24,20},{28,24},{1,29},{... | collective-permute-start | bytes 626696 | tf_op jit(solution)/shard_map/ppermute | solution.py:28
  164.6 2.3 collective-permute-done.6
  168.0 1.6 constant_dynamic-slice_fusion.4
  169.7 2.8 copy.51
  172.5 3.9 %copy.58 = bf16[1088,768]{0,1:T(8,128)(2,1)} copy(bf16[1088,768]{1,0:T(8,128)(2,1)} %all-gather.5.cloned.1.call-done) | data formatting | bytes 3342336 | tf_op jit(solution)/shard_map/all_gather | solution.py:157
  176.3 1.9 select_reduce_fusion
  178.4 65.5 %all-gather.7.cloned.1.call-done = bf16[768,3072]{1,0:T(8,128)(2,1)} async-done(((bf16[768,384]{1,0:T(8,128)(2,1)}), bf16[768,3072]{1,0:T(8,128)(2,1)}) %all-gather.7.cloned.1.call-update) | async-done | bytes 4718608 | tf_op jit(solution)/shard_map/all_gather | solution.py:195
  244.0 3.7 convolution_convert_fusion
  247.6 11.2 %all-reduce = bf16[8,3072]{1,0:T(8,128)(2,1)S(1)} all-reduce(bf16[8,3072]{1,0:T(8,128)(2,1)S(1)} %convolution_convert_fusion), channel_id=2, replica_groups=mesh['row'=8,'col'=4] {'col'}, use_global_device_ids=true, to_apply=%region_11.12.clone | all-reduce | flops 24576 | bytes 98304
  259.3 24.4 %all-gather.1 = bf16[8,2,3072]{2,1,0:T(2,128)(2,1)S(1)} all-gather(bf16[1,2,3072]{2,1,0:T(2,128)(2,1)S(1)} %fusion.51), channel_id=1, replica_groups=mesh['row'=8,'col'=4] {'row'}, dimensions={0}, use_global_device_ids=true | all-gather | bytes 110592 | tf_op jit(solution)/shard_map/all_gather | solution.py:202
  283.8 9.6 %fusion.22 = f32[16,3072]{1,0:T(8,128)} fusion(bf16[1536,3072]{1,0:T(8,128)(2,1)} %param.28, bf16[16,3072]{1,0:T(8,128)(2,1)S(1)} %reshape.272, bf16[3072,1536]{1,0:T(8,128)(2,1)} %param.27), kind=kOutput, calls=%fused_computation.36 | convolution fusion | flops 302211072 | bytes 19169280 | tf_op jit(solution)/shard_map/dot_general | solution.py:206
  294.7 71.4 %all-reduce.3.cloned.1.call-done = f32[16,3072]{1,0:T(8,128)} async-done(((f32[16,3072]{1,0:T(8,128)}), f32[16,3072]{1,0:T(8,128)}) %all-reduce.3.cloned.1.call-update) | async-done | bytes 196624 | tf_op jit(solution)/shard_map/psum | solution.py:207
  366.1 1.0 fusion.82
  367.7 5.6 %collective-permute-start.7 = (f32[1,64]{1,0:T(1,128)S(1)}, f32[1,64]{1,0:T(1,128)S(1)}, u32[]{:S(2)}, u32[]{:S(2)}) collective-permute-start(f32[1,64]{1,0:T(1,128)S(1)} %get-tuple-element.45), channel_id=1, source_target_pairs={{0,1},{1,2},{2,3},{4,5},{5,6},{6,7},{8,9},{9,10},{10,11},{12,13},{... | collective-permute-start | bytes 776 | tf_op jit(solution)/shard_map/ppermute | solution.py:45
  373.2 1.9 collective-permute-start.8
  375.2 2.9 collective-permute-done.8
  (129 shorter events, 25.2 us)
Async XLA Ops:
  7.2 360.2 %copy-start = (bf16[3072,64]{0,1:T(8,128)(2,1)S(1)}, bf16[3072,64]{0,1:T(8,128)(2,1)}, u32[]{:S(2)}) copy-start(bf16[3072,64]{0,1:T(8,128)(2,1)} %param.29) | copy-start | bytes 1179652
  41.0 9.8 %copy-start.12 = (s32[4,2]{0,1:T(2,128)S(1)}, s32[4,2]{0,1:T(2,128)}, u32[]{:S(2)}) copy-start(s32[4,2]{0,1:T(2,128)} %param.21) | copy-start | bytes 100
  41.0 9.8 %copy-start.13 = (s32[4,2]{0,1:T(2,128)S(1)}, s32[4,2]{0,1:T(2,128)}, u32[]{:S(2)}) copy-start(s32[4,2]{0,1:T(2,128)} %param.22) | copy-start | bytes 100
  41.0 12.2 %copy-start.15 = (f32[128]{0:T(128)S(1)}, f32[128]{0:T(128)}, u32[]{:S(2)}) copy-start(f32[128]{0:T(128)} %param.24) | copy-start | bytes 1540
  41.0 12.9 %copy-start.16 = (f32[128]{0:T(128)S(1)}, f32[128]{0:T(128)}, u32[]{:S(2)}) copy-start(f32[128]{0:T(128)} %param.25) | copy-start | bytes 1540
  45.7 10.6 %all-to-all-start = ((bf16[8,2,1152]{2,1,0:T(2,128)(2,1)}), bf16[8,2,1152]{2,1,0:T(2,128)(2,1)S(1)}, u32[]{:S(2)}, u32[]{:S(2)}) async-start(bf16[8,2,1152]{2,1,0:T(2,128)(2,1)} %all_to_all.50), calls=%async_computation | async-start | bytes 73728 | tf_op jit(solution)/shard_map/all_to_all | solution.py:137
  50.7 121.7 %all-gather.5.cloned.1.call-start = ((), (), s32[]{:S(2)}) async-start(), calls=%async_computation.4 | async-start | bytes 1880064 | tf_op jit(solution)/shard_map/all_gather | solution.py:157
  102.6 141.3 %all-gather.7.cloned.1.call-start = ((), (), s32[]{:S(2)}) async-start(), calls=%async_computation.5 | async-start | bytes 5308416 | tf_op jit(solution)/shard_map/all_gather | solution.py:195
  103.4 7.1 %all-to-all-start.1 = ((bf16[2,4,768]{2,0,1:T(2,128)(2,1)}), bf16[2,4,768]{2,0,1:T(2,128)(2,1)S(1)}, u32[]{:S(2)}, u32[]{:S(2)}) async-start(bf16[2,4,768]{2,0,1:T(2,128)(2,1)} %bitcast.72), calls=%async_computation.1 | async-start | bytes 24576 | tf_op jit(solution)/shard_map/all_to_all | solution.py:148
  110.5 0.6 copy-start.7
  114.0 11.6 %collective-permute-start = (bf16[136,768]{1,0:T(8,128)(2,1)}, bf16[136,768]{1,0:T(8,128)(2,1)}, u32[]{:S(2)}, u32[]{:S(2)}) collective-permute-start(bf16[136,768]{1,0:T(8,128)(2,1)} %constant_dynamic-update-slice_fusion), channel_id=1, source_target_pairs={{0,4},{4,8},{8,12},{12,16},{16,20},{20,24},{24,28},{28,0},{1,5},{5... | collective-permute-start | bytes 626696 | tf_op jit(solution)/shard_map/ppermute | solution.py:26
  118.1 32.5 %copy-start.17 = (u32[32]{0:T(128)S(1)}, u32[32]{0:T(128)}, u32[]{:S(2)}) copy-start(u32[32]{0:T(128)} %constant.178) | copy-start | bytes 388
  121.8 28.7 %copy-start.8 = (s32[1088]{0:T(1024)S(1)}, s32[1088]{0:T(1024)}, u32[]{:S(2)}) copy-start(s32[1088]{0:T(1024)} %get-tuple-element.2) | copy-start | bytes 13060
  121.8 28.7 %copy-start.9 = (s32[1088]{0:T(1024)S(1)}, s32[1088]{0:T(1024)}, u32[]{:S(2)}) copy-start(s32[1088]{0:T(1024)} %get-tuple-element.3) | copy-start | bytes 13060
  121.8 42.7 %copy-start.1 = (bf16[128,768]{1,0:T(8,128)(2,1)S(1)}, bf16[128,768]{1,0:T(8,128)(2,1)}, u32[]{:S(2)}) copy-start(bf16[128,768]{1,0:T(8,128)(2,1)} %param.18) | copy-start | bytes 589828
  125.6 9.2 %collective-permute-start.1 = (bf16[136,768]{1,0:T(8,128)(2,1)}, bf16[136,768]{1,0:T(8,128)(2,1)S(1)}, u32[]{:S(2)}, u32[]{:S(2)}) collective-permute-start(bf16[136,768]{1,0:T(8,128)(2,1)} %collective-permute-done), channel_id=1, source_target_pairs={{0,4},{4,8},{8,12},{12,16},{16,20},{20,24},{24,28},{28,0},{1,5},{5... | collective-permute-start | bytes 626696 | tf_op jit(solution)/shard_map/ppermute | solution.py:26
  126.4 22.1 %collective-permute-start.4 = (bf16[136,768]{1,0:T(8,128)(2,1)}, bf16[136,768]{1,0:T(8,128)(2,1)S(1)}, u32[]{:S(2)}, u32[]{:S(2)}) collective-permute-start(bf16[136,768]{1,0:T(8,128)(2,1)} %constant_dynamic-update-slice_fusion), channel_id=1, source_target_pairs={{0,28},{4,0},{8,4},{12,8},{16,12},{20,16},{24,20},{28,24},{1,29},{... | collective-permute-start | bytes 626696 | tf_op jit(solution)/shard_map/ppermute | solution.py:28
  134.8 15.7 %collective-permute-start.2 = (bf16[136,768]{1,0:T(8,128)(2,1)S(1)}, bf16[136,768]{1,0:T(8,128)(2,1)S(1)}, u32[]{:S(2)}, u32[]{:S(2)}) collective-permute-start(bf16[136,768]{1,0:T(8,128)(2,1)S(1)} %collective-permute-done.1), channel_id=1, source_target_pairs={{0,4},{4,8},{8,12},{12,16},{16,20},{20,24},{24,28},{28,0},{1,5},{5... | collective-permute-start | bytes 626696 | tf_op jit(solution)/shard_map/ppermute | solution.py:26
  138.7 13.3 %all-to-all-start.3 = ((bf16[2,4,768]{2,0,1:T(2,128)(2,1)}), bf16[2,4,768]{2,0,1:T(2,128)(2,1)S(1)}, u32[]{:S(2)}, u32[]{:S(2)}) async-start(bf16[2,4,768]{2,0,1:T(2,128)(2,1)} %copy.64), calls=%async_computation.3 | async-start | bytes 24576 | tf_op jit(solution)/shard_map/all_to_all | solution.py:146
  148.5 217.6 %all-reduce.3.cloned.1.call-start = ((), (), s32[]{:S(2)}) async-start(), calls=%async_computation.6 | async-start | bytes 393216 | tf_op jit(solution)/shard_map/psum | solution.py:207
  148.5 10.1 %collective-permute-start.5 = (bf16[136,768]{1,0:T(8,128)(2,1)S(1)}, bf16[136,768]{1,0:T(8,128)(2,1)S(1)}, u32[]{:S(2)}, u32[]{:S(2)}) collective-permute-start(bf16[136,768]{1,0:T(8,128)(2,1)S(1)} %collective-permute-done.4), channel_id=1, source_target_pairs={{0,28},{4,0},{8,4},{12,8},{16,12},{20,16},{24,20},{28,24},{1,29},{... | collective-permute-start | bytes 626696 | tf_op jit(solution)/shard_map/ppermute | solution.py:28
  150.5 13.0 %collective-permute-start.3 = (bf16[136,768]{1,0:T(8,128)(2,1)S(1)}, bf16[136,768]{1,0:T(8,128)(2,1)S(1)}, u32[]{:S(2)}, u32[]{:S(2)}) collective-permute-start(bf16[136,768]{1,0:T(8,128)(2,1)S(1)} %collective-permute-done.2), channel_id=1, source_target_pairs={{0,4},{4,8},{8,12},{12,16},{16,20},{20,24},{24,28},{28,0},{1,5},{5... | collective-permute-start | bytes 626696 | tf_op jit(solution)/shard_map/ppermute | solution.py:26
  158.6 8.3 %collective-permute-start.6 = (bf16[136,768]{1,0:T(8,128)(2,1)S(1)}, bf16[136,768]{1,0:T(8,128)(2,1)S(1)}, u32[]{:S(2)}, u32[]{:S(2)}) collective-permute-start(bf16[136,768]{1,0:T(8,128)(2,1)S(1)} %collective-permute-done.5), channel_id=1, source_target_pairs={{0,28},{4,0},{8,4},{12,8},{16,12},{20,16},{24,20},{28,24},{1,29},{... | collective-permute-start | bytes 626696 | tf_op jit(solution)/shard_map/ppermute | solution.py:28
  244.0 14.9 %copy-start.2 = (bf16[2,3072]{1,0:T(2,128)(2,1)S(1)}, bf16[2,3072]{1,0:T(2,128)(2,1)}, u32[]{:S(2)}) copy-start(bf16[2,3072]{1,0:T(2,128)(2,1)} %param.15) | copy-start | bytes 36868
  244.0 14.9 %copy-start.6 = (f32[1,1,3072]{2,1,0:T(1,128)S(1)}, f32[1,1,3072]{2,1,0:T(1,128)}, u32[]{:S(2)}) copy-start(f32[1,1,3072]{2,1,0:T(1,128)} %get-tuple-element.30) | copy-start | bytes 36868
  244.0 15.3 %copy-start.4 = (f32[1,1,3072]{2,1,0:T(1,128)S(1)}, f32[1,1,3072]{2,1,0:T(1,128)}, u32[]{:S(2)}) copy-start(f32[1,1,3072]{2,1,0:T(1,128)} %get-tuple-element.25) | copy-start | bytes 36868
  244.0 15.3 %copy-start.5 = (f32[1,1,3072]{2,1,0:T(1,128)S(1)}, f32[1,1,3072]{2,1,0:T(1,128)}, u32[]{:S(2)}) copy-start(f32[1,1,3072]{2,1,0:T(1,128)} %get-tuple-element.26) | copy-start | bytes 36868
  283.8 82.3 %copy-start.3 = (f32[1,1,3072]{2,1,0:T(1,128)S(1)}, f32[1,1,3072]{2,1,0:T(1,128)}, u32[]{:S(2)}) copy-start(f32[1,1,3072]{2,1,0:T(1,128)} %get-tuple-element.27) | copy-start | bytes 36868
  283.8 83.6 %copy-start.10 = (f32[1,1,3072]{2,1,0:T(1,128)S(1)}, f32[1,1,3072]{2,1,0:T(1,128)}, u32[]{:S(2)}) copy-start(f32[1,1,3072]{2,1,0:T(1,128)} %get-tuple-element.24) | copy-start | bytes 36868
  283.8 83.6 %copy-start.11 = (f32[1,1,3072]{2,1,0:T(1,128)S(1)}, f32[1,1,3072]{2,1,0:T(1,128)}, u32[]{:S(2)}) copy-start(f32[1,1,3072]{2,1,0:T(1,128)} %get-tuple-element.31) | copy-start | bytes 36868
  283.8 94.3 %copy-start.14 = (f32[2,64]{1,0:T(2,128)S(1)}, f32[2,64]{1,0:T(2,128)}, u32[]{:S(2)}) copy-start(f32[2,64]{1,0:T(2,128)} %param.16) | copy-start | bytes 1540
  367.7 7.5 %collective-permute-start.7 = (f32[1,64]{1,0:T(1,128)S(1)}, f32[1,64]{1,0:T(1,128)S(1)}, u32[]{:S(2)}, u32[]{:S(2)}) collective-permute-start(f32[1,64]{1,0:T(1,128)S(1)} %get-tuple-element.45), channel_id=1, source_target_pairs={{0,1},{1,2},{2,3},{4,5},{5,6},{6,7},{8,9},{9,10},{10,11},{12,13},{... | collective-permute-start | bytes 776 | tf_op jit(solution)/shard_map/ppermute | solution.py:45
  373.2 4.9 %collective-permute-start.8 = (f32[1,64]{1,0:T(1,128)S(1)}, f32[1,64]{1,0:T(1,128)S(1)}, u32[]{:S(2)}, u32[]{:S(2)}) collective-permute-start(f32[1,64]{1,0:T(1,128)S(1)} %get-tuple-element.46), channel_id=1, source_target_pairs={{1,0},{2,1},{3,2},{5,4},{6,5},{7,6},{9,8},{10,9},{11,10},{13,12},{... | collective-permute-start | bytes 776 | tf_op jit(solution)/shard_map/ppermute | solution.py:47
Sparse Core Ops, SparseCore 0:
  102.8 58.0 all-gather.4
  162.9 81.0 all-gather.6
  293.6 72.4 all-reduce.2
